TPU v7x, 256 devices: a whole 4x4x8 slice. The times are simulated.
256 devices in a mesh: feat: 32 (over y, z), dp: 8 (over x, core).
Axes of the slice: x: 4, y: 4, z: 8, core: 2. Of those that a mesh axis runs over, the one named last changes fastest.
Arguments:
- query_grads: bfloat16 [512, 131072], P(('dp', 'feat')), may hold values from -52 to 52
- build_grads: bfloat16 [1024, 131072], P('dp', 'feat'), may hold values from -52 to 52
- scored_grads: bfloat16 [4096, 131072], P('dp', 'feat'), may hold values from -52 to 52
Outputs:
- scores: float32 [4096, 512], P(('dp', 'feat'))
All inputs are finite; a program needn't handle non-finite values.
Results may differ from a plain program's by a relative error of at most 0.0049.
Values may be sent and summed in bfloat16 or wider, within the bound.
No kernel may reach another device: no remote copies, remote signals or barrier semaphores. Data moves between devices by JAX's collectives and lax.ppermute only.
A program may use at most 128 MiB of HBM per device.

v0:
```python
import functools

import jax
import jax.numpy as jnp
from jax import lax
from jax.sharding import Mesh
from jax.sharding import PartitionSpec as P

FEAT = 131072
FEAT_AXES = ("feat_0", "feat_1")
DP = ("dp_0", "dp_1")
FEAT_DP = ("feat_0", "feat_1", "dp_0", "dp_1")
DP_FEAT = ("dp_0", "dp_1", "feat_0", "feat_1")


def one_axis_at_a_time(shard, axes):
    return functools.reduce(lax.psum, axes, shard)


def sent_to_all(shard, axis):
    size = lax.axis_size(axis)
    return lax.all_to_all(
        jnp.broadcast_to(shard[None], (size, *shard.shape)), axis, 0, 0, tiled=True
    )


def taken_together(shard, axis):
    everything = sent_to_all(shard, axis)
    return jnp.sum(everything, axis=0)


def split_up(shard, dim, size):
    before, after = (shard.shape[:dim], shard.shape[dim + 1 :])
    return jnp.moveaxis(shard.reshape(*before, size, -1, *after), dim, 0)


def sent_and_summed(shard, axis, dim):
    size = lax.axis_size(axis)
    blocks = lax.all_to_all(split_up(shard, dim, size), axis, 0, 0, tiled=True)
    return jnp.sum(blocks, axis=0)


def contract_last(left, right):
    return lax.dot_general(
        left, right, (((1,), (1,)), ((), ())), preferred_element_type=jnp.float32
    )


def on_device(query_grads, build_grads, scored_grads):
    q_local = lax.all_to_all(query_grads, FEAT_AXES, split_axis=1, concat_axis=0, tiled=True)
    gathered = lax.all_gather(build_grads, DP, axis=0, tiled=True)
    build_count = gathered.shape[0]
    cross_part = contract_last(gathered, q_local)
    gram_part = contract_last(gathered, gathered)
    gram_matrix, cross_sums = lax.psum((gram_part, cross_part), FEAT_AXES)
    build_wide = build_grads.astype(jnp.float32)
    square_total = one_axis_at_a_time(jnp.sum(build_wide * build_wide), FEAT_DP)
    damping = 0.1 * square_total / (build_count * FEAT) + 1e-06
    gram_matrix = gram_matrix + build_count * damping * jnp.eye(build_count, dtype=jnp.float32)
    factor = jnp.linalg.cholesky(gram_matrix)
    solved = jax.scipy.linalg.cho_solve((factor, True), cross_sums)
    solved_half = solved.astype(jnp.bfloat16)
    query_wide = q_local.astype(jnp.float32)
    removed = lax.dot_general(
        solved_half, gathered, (((0,), (0,)), ((), ())), preferred_element_type=jnp.float32
    )
    precond = (query_wide - removed) / damping
    self_score = taken_together(jnp.sum(query_wide * precond, axis=1), FEAT_AXES)
    normed = (precond / jnp.sqrt(self_score)[:, None]).astype(jnp.bfloat16)
    partial_value = contract_last(scored_grads, lax.all_gather(normed, DP, axis=0, tiled=True))
    return sent_and_summed(partial_value, FEAT_AXES, 0)


def solution(mesh):
    torus = Mesh(mesh.devices.reshape(4, 8, 4, 2), ("feat_0", "feat_1", "dp_0", "dp_1"))
    in_specs = (P(DP_FEAT, None), P(DP, FEAT_AXES), P(DP, FEAT_AXES))
    out_specs = P(DP_FEAT, None)
    return jax.shard_map(
        on_device, mesh=torus, in_specs=in_specs, out_specs=out_specs, check_vma=False
    )
```

profile of v0, /device:TPU:32, one launch (start us, length us, event | category | flops | bytes accessed | tf_op | source)
XLA Modules:
  0.0 705.6 jit_solution(6234472942404162147)
XLA Ops:
  7.3 29.0 %all_to_all.30 = bf16[2,32,4096]{2,0,1:T(2,128)(2,1)S(1)} all-to-all(bf16[2,32,4096]{2,0,1:T(2,128)(2,1)} %bitcast.141), channel_id=1, replica_groups=mesh['feat_0'=4,'feat_1'=8,'dp_0'=4,'dp_1'=2] {'feat_0','feat_1'}, dimensions={1} | all-to-all | bytes 1048576 | tf_op jit(solution)/shard_map/all_to_all | solution.py:50
  36.5 27.5 %all-gather.3.cloned.1.call-done = bf16[1024,4096]{1,0:T(8,128)(2,1)} async-done(((bf16[128,4096]{1,0:T(8,128)(2,1)}), bf16[1024,4096]{1,0:T(8,128)(2,1)}) %all-gather.3.cloned.1.call-update) | async-done | bytes 8388624 | tf_op jit(solution)/shard_map/all_gather | solution.py:51
  64.0 16.0 %fusion.97 = f32[1024,1024]{0,1:T(8,128)} fusion(bf16[1024,4096]{1,0:T(8,128)(2,1)} %all-gather.3.cloned.1.call-done), kind=kOutput, calls=%fused_computation.222 | convolution fusion | flops 8589934592 | bytes 12582912 | tf_op jit(solution)/shard_map/dot_general | solution.py:44
  80.0 3.4 fusion.98
  85.7 11.1 %psum.43 = f32[]{:T(128)} all-reduce(f32[]{:T(128)} %multiply_reduce_fusion), channel_id=1, replica_groups=mesh['feat_0'=4,'feat_1'=8,'dp_0'=4,'dp_1'=2] {'feat_0'}, use_global_device_ids=true, to_apply=%region_2.0 | all-reduce | flops 1 | bytes 8 | tf_op jit(solution)/shard_map/psum | solution.py:17
  96.8 16.9 %psum.44 = f32[]{:T(128)} all-reduce(f32[]{:T(128)} %psum.43), channel_id=1, replica_groups=mesh['feat_0'=4,'feat_1'=8,'dp_0'=4,'dp_1'=2] {'feat_1'}, use_global_device_ids=true, to_apply=%region_3.0 | all-reduce | flops 1 | bytes 8 | tf_op jit(solution)/shard_map/psum | solution.py:17
  113.7 9.3 %psum.45 = f32[]{:T(128)} all-reduce(f32[]{:T(128)} %psum.44), channel_id=1, replica_groups=mesh['feat_0'=4,'feat_1'=8,'dp_0'=4,'dp_1'=2] {'dp_0'}, use_global_device_ids=true, to_apply=%region_4.0 | all-reduce | flops 1 | bytes 8 | tf_op jit(solution)/shard_map/psum | solution.py:17
  123.0 3.1 psum.46
  126.7 122.8 %all-reduce.4.cloned.1.call-done = (f32[1024,1024]{0,1:T(8,128)}, f32[1024,64]{0,1:T(8,128)}) async-done(((f32[1024,1024]{0,1:T(8,128)}, f32[1024,64]{0,1:T(8,128)}), (f32[1024,1024]{0,1:T(8,128)}, f32[1024,64]{0,1:T(8,128)})) %all-reduce.4.cloned.1.call-update) | async-done | bytes 4456464 | tf_op jit(solution)/shard_map/psum | solution.py:55
  249.5 4.8 select_add_fusion
  254.3 5.8 copy.44
  260.1 4.5 fusion
  264.6 2.0 copy-done.2
  266.6 11.7 %cholesky.222 = f32[128,128]{1,0:T(8,128)S(1)} custom-call(f32[128,128]{1,0:T(8,128)S(1)} %cholesky.577), custom_call_target="Cholesky" | custom-call | tf_op jit(solution)/shard_map/jit(cholesky)/cholesky | solution.py:60
  278.4 9.8 %custom-call.66 = f32[1,128,128]{1,2,0:T(8,128)S(1)} custom-call(f32[1,128,128]{2,1,0:T(8,128)S(1)} %get-tuple-element.50), custom_call_target="InvertDiagBlocksLowerTriangular" | custom-call | tf_op jit(solution)/shard_map/jit(cholesky)/cholesky | solution.py:60
  288.2 1.5 fusion.11
  290.0 1.6 convolution_subtract_fusion.1
  291.5 11.7 %cholesky.243 = f32[128,128]{1,0:T(8,128)S(1)} custom-call(f32[128,128]{1,0:T(8,128)S(1)} %cholesky.581), custom_call_target="Cholesky" | custom-call | tf_op jit(solution)/shard_map/jit(cholesky)/cholesky | solution.py:60
  303.5 9.8 %custom-call.67 = f32[1,128,128]{1,2,0:T(8,128)S(1)} custom-call(f32[1,128,128]{2,1,0:T(8,128)S(1)} %get-tuple-element.48), custom_call_target="InvertDiagBlocksLowerTriangular" | custom-call | tf_op jit(solution)/shard_map/jit(cholesky)/cholesky | solution.py:60
  314.5 1.9 copy-done.1
  316.4 2.4 convolution_subtract_fusion.2
  318.9 11.7 %cholesky.466 = f32[128,128]{1,0:T(8,128)S(1)} custom-call(f32[128,128]{1,0:T(8,128)S(1)} %cholesky.586), custom_call_target="Cholesky" | custom-call | tf_op jit(solution)/shard_map/jit(cholesky)/cholesky | solution.py:60
  331.3 9.8 %custom-call.68 = f32[1,128,128]{1,2,0:T(8,128)S(1)} custom-call(f32[1,128,128]{2,1,0:T(8,128)S(1)} %get-tuple-element.46), custom_call_target="InvertDiagBlocksLowerTriangular" | custom-call | tf_op jit(solution)/shard_map/jit(cholesky)/cholesky | solution.py:60
  341.2 1.2 convolution_dynamic-update-slice_fusion.1
  342.4 3.3 convolution_subtract_fusion.3
  345.7 11.7 %cholesky.485 = f32[128,128]{1,0:T(8,128)S(1)} custom-call(f32[128,128]{1,0:T(8,128)S(1)} %cholesky.591), custom_call_target="Cholesky" | custom-call | tf_op jit(solution)/shard_map/jit(cholesky)/cholesky | solution.py:60
  358.2 9.8 %custom-call.69 = f32[1,128,128]{1,2,0:T(8,128)S(1)} custom-call(f32[1,128,128]{2,1,0:T(8,128)S(1)} %get-tuple-element.44), custom_call_target="InvertDiagBlocksLowerTriangular" | custom-call | tf_op jit(solution)/shard_map/jit(cholesky)/cholesky | solution.py:60
  369.2 3.2 convolution_subtract_fusion.4
  372.3 12.1 %cholesky.504 = f32[128,128]{1,0:T(8,128)S(1)} custom-call(f32[128,128]{1,0:T(8,128)S(1)} %cholesky.596), custom_call_target="Cholesky" | custom-call | tf_op jit(solution)/shard_map/jit(cholesky)/cholesky | solution.py:60
  385.2 9.8 %custom-call.70 = f32[1,128,128]{1,2,0:T(8,128)S(1)} custom-call(f32[1,128,128]{2,1,0:T(8,128)S(1)} %get-tuple-element.42), custom_call_target="InvertDiagBlocksLowerTriangular" | custom-call | tf_op jit(solution)/shard_map/jit(cholesky)/cholesky | solution.py:60
  396.2 3.1 convolution_subtract_fusion.5
  399.3 11.7 %cholesky.524 = f32[128,128]{1,0:T(8,128)S(1)} custom-call(f32[128,128]{1,0:T(8,128)S(1)} %cholesky.601), custom_call_target="Cholesky" | custom-call | tf_op jit(solution)/shard_map/jit(cholesky)/cholesky | solution.py:60
  411.8 9.8 %custom-call.71 = f32[1,128,128]{1,2,0:T(8,128)S(1)} custom-call(f32[1,128,128]{2,1,0:T(8,128)S(1)} %get-tuple-element.40), custom_call_target="InvertDiagBlocksLowerTriangular" | custom-call | tf_op jit(solution)/shard_map/jit(cholesky)/cholesky | solution.py:60
  422.6 2.8 convolution_subtract_fusion.6
  425.4 11.7 %cholesky.544 = f32[128,128]{1,0:T(8,128)S(1)} custom-call(f32[128,128]{1,0:T(8,128)S(1)} %cholesky.606), custom_call_target="Cholesky" | custom-call | tf_op jit(solution)/shard_map/jit(cholesky)/cholesky | solution.py:60
  437.9 9.8 %custom-call.72 = f32[1,128,128]{1,2,0:T(8,128)S(1)} custom-call(f32[1,128,128]{2,1,0:T(8,128)S(1)} %get-tuple-element.38), custom_call_target="InvertDiagBlocksLowerTriangular" | custom-call | tf_op jit(solution)/shard_map/jit(cholesky)/cholesky | solution.py:60
  448.6 2.1 convolution_subtract_fusion.7
  450.7 11.7 %cholesky.562 = f32[128,128]{1,0:T(8,128)S(1)} custom-call(f32[128,128]{1,0:T(8,128)S(1)} %convolution_subtract_fusion.7), custom_call_target="Cholesky" | custom-call | tf_op jit(solution)/shard_map/jit(cholesky)/cholesky | solution.py:60
  472.7 4.9 select_select_fusion
  477.6 24.0 %while.1 = (s32[]{:T(128)}, f32[1024,1024]{0,1:T(8,128)}, s32[8,2]{0,1:T(2,128)S(1)}, f32[8,128,128]{2,1,0:T(8,128)S(1)}, s32[]{:T(128)}) while((s32[]{:T(128)}, f32[1024,1024]{0,1:T(8,128)}, s32[8,2]{0,1:T(2,128)S(1)}, f32[8,128,128]{2,1,0:T(8,128)S(1)}, s32[]{:T(128)}) %tuple.53), condition=%wide.while_cond, body=%wide.while_body.sunk | while | flops 2 | bytes 393329 | solution.py:61
  478.2 2.3 dynamic-slice.7
  481.2 2.3 dynamic-slice.7
  484.2 2.3 dynamic-slice.7
  487.2 2.3 dynamic-slice.7
  490.2 2.3 dynamic-slice.7
  493.2 2.3 dynamic-slice.7
  496.2 2.3 dynamic-slice.7
  499.2 2.2 dynamic-slice.7
  501.5 78.8 %custom-call.73 = f32[8,128,128]{1,2,0:T(8,128)S(1)} custom-call(f32[8,128,128]{2,1,0:T(8,128)S(1)} %get-tuple-element.12), custom_call_target="InvertDiagBlocksLowerTriangular" | custom-call | tf_op jit(solution)/shard_map/jit(_cho_solve)/triangular_solve | solution.py:61
  583.1 1.2 convolution_subtract_fusion.13
  584.5 1.2 convolution_subtract_fusion.21
  585.9 1.3 convolution_subtract_fusion.20
  587.4 1.4 convolution_subtract_fusion.19
  589.0 1.4 convolution_subtract_fusion.12
  593.6 1.3 convolution_subtract_fusion.9
  595.2 1.4 convolution_subtract_fusion.18
  596.9 1.5 convolution_subtract_fusion.17
  598.6 1.5 convolution_subtract_fusion.16
  600.5 1.7 convolution_subtract_fusion.8
  602.5 5.2 fusion.2
  607.7 14.9 %all_to_all.31 = f32[32,1,64]{2,1,0:T(1,128)S(1)} all-to-all(f32[32,1,64]{2,1,0:T(1,128)S(1)} %broadcast_in_dim.4), channel_id=1, replica_groups=mesh['feat_0'=4,'feat_1'=8,'dp_0'=4,'dp_1'=2] {'feat_0','feat_1'}, dimensions={0} | all-to-all | bytes 16384 | tf_op jit(solution)/shard_map/all_to_all | solution.py:22
  623.6 30.1 %all-gather.5.cloned.1.call-done = bf16[512,4096]{1,0:T(8,128)(2,1)} async-done(((bf16[64,4096]{1,0:T(8,128)(2,1)}), bf16[512,4096]{1,0:T(8,128)(2,1)}) %all-gather.5.cloned.1.call-update) | async-done | bytes 4194320 | tf_op jit(solution)/shard_map/all_gather | solution.py:70
  653.7 5.8 fusion.99
  659.6 38.6 %all_to_all.32 = f32[32,16,512]{2,1,0:T(8,128)S(1)} all-to-all(f32[32,16,512]{2,1,0:T(8,128)S(1)} %bitcast.140), channel_id=1, replica_groups=mesh['feat_0'=4,'feat_1'=8,'dp_0'=4,'dp_1'=2] {'feat_0','feat_1'}, dimensions={0} | all-to-all | bytes 2097152 | tf_op jit(solution)/shard_map/all_to_all | solution.py:39
  (143 shorter events, 33.8 us)
Async XLA Ops:
  6.5 57.5 %all-gather.3.cloned.1.call-start = ((), (), s32[]{:S(2)}) async-start(), calls=%async_computation.3 | async-start | bytes 9437184 | tf_op jit(solution)/shard_map/all_gather | solution.py:51
  7.3 242.2 %all-reduce.4.cloned.1.call-start = ((), (), s32[]{:S(2)}) async-start(), calls=%async_computation.5 | async-start | bytes 8912896 | tf_op jit(solution)/shard_map/psum | solution.py:55
  64.0 16.0 %copy-start = (bf16[1024,4096]{1,0:T(8,128)(2,1)S(1)}, bf16[1024,4096]{1,0:T(8,128)(2,1)}, u32[]{:S(2)}) copy-start(bf16[1024,4096]{1,0:T(8,128)(2,1)} %all-gather.3.cloned.1.call-done) | copy-start | bytes 25165828
  83.3 1.2 copy-start.3
  83.4 570.4 %all-gather.5.cloned.1.call-start = ((), (), s32[]{:S(2)}) async-start(), calls=%async_computation.4 | async-start | bytes 4718592 | tf_op jit(solution)/shard_map/all_gather | solution.py:70
  264.6 2.0 copy-start.2
  314.5 2.0 copy-start.1
  472.6 107.7 %copy-start.4 = (f32[1024,64]{0,1:T(8,128)S(1)}, f32[1024,64]{0,1:T(8,128)}, u32[]{:S(2)}) copy-start(f32[1024,64]{0,1:T(8,128)} %get-tuple-element.34) | copy-start | bytes 786436
Sparse Core Ops, SparseCore 0:
  9.2 54.7 all-gather.2
  83.5 165.9 all-reduce.3
  623.7 29.9 all-gather.4
where the time goes:
time: 713 us; the launch traced here: 706 us
  other arithmetic  263 us (37%)
  waiting for transfers between devices  181 us (25%)
  blocking collectives  123 us (17%)
  matrix products  77.9 us (11%)
  local copies, waits for them, and re-layouts  40.5 us (6%)
  between operations  19.6 us (3%)
    another operation x30, other arithmetic, on_device(): factor = jnp.linalg.cholesky(gram_matrix)  168 us
    psum x1, waiting for transfers between devices, on_device(): gram_matrix, cross_sums = lax.psum((gram_part, cross_part), FEAT_AXES)  123 us
    another operation x4, other arithmetic, on_device(): solved = jax.scipy.linalg.cho_solve((factor, True), cross_sums)  83.7 us
    psum x4, blocking collectives, one_axis_at_a_time(): return functools.reduce(lax.psum, axes, shard)  40.4 us
    all_to_all x1, blocking collectives, sent_and_summed(): blocks = lax.all_to_all(split_up(shard, dim, size), axis, 0, 0, tiled=True)  38.6 us
    all_gather x1, waiting for transfers between devices, on_device(): lax.all_gather(normed, DP, axis=0, tiled=True)  30.1 us
    all_to_all x1, blocking collectives, on_device(): lax.all_to_all(query_grads, FEAT_AXES, split_axis=1, concat_axis=0, tiled...  29 us
    all_gather x1, waiting for transfers between devices, on_device(): gathered = lax.all_gather(build_grads, DP, axis=0, tiled=True)  27.5 us
  transfers between devices with their start and end apart: 3, of which 3 were waited for; matrix products, arithmetic and copies ran while one was open for 0% of the time, Pallas kernels for 0%

commit v1 on v0

v1 whole, which is shorter than its diff:
```python
import functools
import jax, jax.numpy as jnp
from jax import lax
from jax.experimental import pallas as pl
from jax.experimental.pallas import tpu as pltpu

BLK = 128
BF = jnp.bfloat16
F32 = jnp.float32

def split3(x):
    h = x.astype(BF)
    r = x - h.astype(F32)
    m = r.astype(BF)
    l = (r - m.astype(F32)).astype(BF)
    return h, m, l

def cat_left(x):
    h, m, l = split3(x)
    return jnp.concatenate([h, h, m, h, l, m], axis=1)

def cat_right(x):
    h, m, l = split3(x)
    return jnp.concatenate([h, m, h, l, h, m], axis=0)

def mm(a, b):
    return jnp.dot(a, b, preferred_element_type=F32)

def inverse(a):
    n = a.shape[0]
    lane = lax.broadcasted_iota(jnp.int32, (1, n), 1)
    for j in range(0, n, 2):
        c0 = jnp.broadcast_to(a[:, j:j+1], (n, n))
        c1 = jnp.broadcast_to(a[:, j+1:j+2], (n, n))
        p, q, s = c0[j:j+1], c0[j+1:j+2], c1[j+1:j+2]
        inv = 1.0 / (p * s - q * q)
        i00, i01, i11 = s * inv, -q * inv, p * inv
        r0 = jnp.where(lane == j, 1.0, jnp.where(lane == j + 1, 0.0, a[j:j+1]))
        r1 = jnp.where(lane == j, 0.0, jnp.where(lane == j + 1, 1.0, a[j+1:j+2]))
        t0 = i00 * r0 + i01 * r1
        t1 = i01 * r0 + i11 * r1
        keep = (lane == j) | (lane == j + 1)
        base = jnp.where(keep, 0.0, a)
        new = base - c0 * t0 - c1 * t1
        parts = []
        if j: parts.append(new[:j])
        parts += [t0, t1]
        if j + 2 < n: parts.append(new[j+2:])
        a = jnp.concatenate(parts, axis=0)
    return a

def solve_kernel(n, nq, m_ref, x_ref, dots_ref, damp_ref, a, t, dinv, w, lc):
    g = n // BLK
    qs = nq // g
    tot = jnp.zeros((BLK, BLK), F32)
    eye = (lax.broadcasted_iota(jnp.int32, (BLK, BLK), 0) == lax.broadcasted_iota(jnp.int32, (BLK, BLK), 1)).astype(F32)
    for k in range(g):
        for c in range(n // 256):
            a[k*BLK:(k+1)*BLK, c*256:(c+1)*256] = m_ref[k, c, :BLK, :]
            t[k*qs:(k+1)*qs, c*256:(c+1)*256] = m_ref[k, c, BLK:, :]
        tot = tot + a[k*BLK:(k+1)*BLK, k*BLK:(k+1)*BLK] * eye
    trace = jnp.sum(jnp.sum(tot, axis=1, keepdims=True), axis=0, keepdims=True)
    damping = 0.1 * trace / (n * 131072) + 1e-06
    damp_ref[...] = jnp.broadcast_to(damping, (8, 128))
    for k in range(g):
        s = slice(k*BLK, (k+1)*BLK)
        a[s, s] = a[s, s] + eye * (n * damping)
    tiles = n // 256

    def update(ref, rt, ct):
        rs = pl.ds(pl.multiple_of(rt * 256, 256), 256)
        cs = pl.ds(pl.multiple_of(ct * 256, 256), 256)
        ref[rs, cs] = ref[rs, cs] - mm(lc[rs, :], w[:, cs])

    def set_left(ref, rt, ks):
        rs = pl.ds(pl.multiple_of(rt * 256, 256), 256)
        lc[rs, :] = cat_left(ref[rs, ks])

    col = lax.broadcasted_iota(jnp.int32, (1, n), 1)

    def forward(k, _):
        ks = pl.ds(pl.multiple_of(k * BLK, BLK), BLK)
        d = inverse(a[ks, ks])
        dinv[ks, :] = d
        lo = (k + 1) // 2
        dl = cat_left(d)
        def make_w(ct, _):
            cs = pl.ds(pl.multiple_of(ct * 256, 256), 256)
            cc = lax.broadcasted_iota(jnp.int32, (1, 256), 1) + ct * 256
            v = mm(dl, cat_right(a[ks, cs]))
            w[:, cs] = cat_right(jnp.where(cc >= (k + 1) * BLK, v, 0.0))
            return 0
        lax.fori_loop(lo, tiles, make_w, 0)
        def rows_a(rt, _):
            set_left(a, rt, ks)
            def cols(ct, _):
                update(a, rt, ct)
                return 0
            return lax.fori_loop(lo, tiles, cols, 0)
        lax.fori_loop(lo, tiles, rows_a, 0)
        def rows_t(rt, _):
            set_left(t, rt, ks)
            def cols(ct, _):
                update(t, rt, ct)
                return 0
            return lax.fori_loop(lo, tiles, cols, 0)
        lax.fori_loop(0, nq // 256, rows_t, 0)
        return 0
    lax.fori_loop(0, g, forward, 0)

    def backward(i, _):
        k = g - 1 - i
        ks = pl.ds(pl.multiple_of(k * BLK, BLK), BLK)
        dr = cat_right(dinv[ks, :])
        hi = (k + 1) // 2
        def make_w(ct, _):
            cs = pl.ds(pl.multiple_of(ct * 256, 256), 256)
            cc = lax.broadcasted_iota(jnp.int32, (1, 256), 1) + ct * 256
            w[:, cs] = cat_right(jnp.where(cc < k * BLK, a[ks, cs], 0.0))
            return 0
        lax.fori_loop(0, hi, make_w, 0)
        def rows_t(rt, _):
            rs = pl.ds(pl.multiple_of(rt * 256, 256), 256)
            x = mm(cat_left(t[rs, ks]), dr)
            t[rs, ks] = x
            lc[rs, :] = cat_left(x)
            def cols(ct, _):
                update(t, rt, ct)
                return 0
            return lax.fori_loop(0, hi, cols, 0)
        lax.fori_loop(0, nq // 256, rows_t, 0)
        return 0
    lax.fori_loop(0, g, backward, 0)
    for k in range(g):
        xs = t[k*qs:(k+1)*qs, :].astype(BF)
        x_ref[k*qs:(k+1)*qs, :] = xs
        acc = jnp.zeros((qs, 256), F32)
        for c in range(n // 256):
            acc = acc + xs[:, c*256:(c+1)*256].astype(F32) * m_ref[k, c, BLK:, :]
        dots_ref[k*qs:(k+1)*qs, :] = jnp.broadcast_to(jnp.sum(acc, axis=1, keepdims=True), (qs, 128))

def solve(m):
    g, chunks, rows, _ = m.shape
    n = chunks * 256
    nq = g * (rows - BLK)
    vm = pl.BlockSpec(memory_space=pltpu.VMEM)
    return pl.pallas_call(
        functools.partial(solve_kernel, n, nq),
        out_shape=(jax.ShapeDtypeStruct((nq, n), BF), jax.ShapeDtypeStruct((nq, 128), F32), jax.ShapeDtypeStruct((8, 128), F32)),
        in_specs=[vm], out_specs=(vm, vm, vm),
        scratch_shapes=[pltpu.VMEM((n, n), F32), pltpu.VMEM((nq, n), F32), pltpu.VMEM((n, BLK), F32),
                        pltpu.VMEM((6*BLK, n), BF), pltpu.VMEM((max(n, nq), 6*BLK), BF)],
        compiler_params=pltpu.CompilerParams(vmem_limit_bytes=56 * 1024 * 1024),
        cost_estimate=pl.CostEstimate(flops=20_000_000_000, bytes_accessed=8_000_000, transcendentals=0),
        name="solve",
    )(m)


from jax.sharding import Mesh
from jax.sharding import PartitionSpec as P

FEAT = 131072
FEAT_AXES = ("feat_0", "feat_1")
DP = ("dp_0", "dp_1")
DP_FEAT = ("dp_0", "dp_1", "feat_0", "feat_1")


def contract_last(left, right):
    return lax.dot_general(left, right, (((1,), (1,)), ((), ())), preferred_element_type=F32)


def on_device(query_grads, build_grads, scored_grads):
    q_local = lax.all_to_all(query_grads, FEAT_AXES, split_axis=1, concat_axis=0, tiled=True)
    build_all = lax.all_gather(build_grads, DP, axis=0, tiled=True)
    rows = jnp.concatenate([build_grads, q_local], axis=0)
    query_wide = q_local.astype(F32)
    own_squares = jnp.sum(query_wide * query_wide, axis=1)
    slot = lax.axis_index(DP)
    squares = jnp.zeros((lax.axis_size(DP), own_squares.shape[0]), F32).at[slot].set(own_squares)
    squares = lax.psum(squares.reshape(-1), FEAT_AXES + DP)
    squares, rows = lax.optimization_barrier((squares, rows))
    build_rows = build_all.shape[0]
    sums = jnp.concatenate([contract_last(rows, build_all[c:c + 256]) for c in range(0, build_rows, 256)], axis=0)
    sums = lax.psum_scatter(sums, FEAT_AXES, scatter_dimension=0, tiled=True)
    score_build = contract_last(scored_grads, build_all)
    high = lax.reduce_precision(score_build, 8, 7)
    low = (score_build - high).astype(BF)
    pair = jnp.concatenate([high.astype(BF), low], axis=1)
    sums, pair = lax.optimization_barrier((sums, pair))
    sums = lax.all_gather(sums, DP_FEAT, axis=0, tiled=True)
    q_local, sums = lax.optimization_barrier((q_local, sums))
    query_all = lax.all_gather(q_local, DP, axis=0, tiled=True)
    half, dots, damp = solve(sums.reshape(build_rows // BLK, build_rows // 256, -1, 256))
    damping = damp[0, 0]
    self_score = (squares - dots[:, 0]) / damping
    scale = 1.0 / (damping * jnp.sqrt(self_score))
    score_query = contract_last(scored_grads, query_all)
    removed = contract_last(pair, jnp.concatenate([half, half], axis=1))
    partial_value = (score_query - removed) * scale[None, :]
    return lax.psum_scatter(partial_value, FEAT_AXES, scatter_dimension=0, tiled=True)


def solution(mesh):
    torus = Mesh(mesh.devices.reshape(4, 8, 4, 2), ("feat_0", "feat_1", "dp_0", "dp_1"))
    in_specs = (P(DP_FEAT, None), P(DP, FEAT_AXES), P(DP, FEAT_AXES))
    out_specs = P(DP_FEAT, None)
    return jax.shard_map(
        on_device, mesh=torus, in_specs=in_specs, out_specs=out_specs, check_vma=False
    )
```

time: 713 us -> 796 us (1.12)
  waiting for transfers between devices: 181 us -> 553 us
  other arithmetic: 263 us -> 5.04 us
  Pallas kernels: 0 us -> 103 us
  matrix products: 77.9 us -> 28.3 us
  blocking collectives: 123 us -> 74.8 us
  local copies, waits for them, and re-layouts: 40.5 us -> 4.02 us
  starting transfers between devices: 0.08 us -> 11.7 us
    reduce_scatter x0 -> x2, waiting for transfers between devices: none -> 417 us  [the longest x1 214 us: on_device(): lax.psum_scatter(partial_value, FEAT_AXES, scatter_dimension=0, tiled=True)]
    another operation x35 -> x2, other arithmetic: 251 us -> 1.39 us  [the longest x30 168 us: on_device(): factor = jnp.linalg.cholesky(gram_matrix)]
    psum x1 -> x0, waiting for transfers between devices: 123 us -> none  [on_device(): gram_matrix, cross_sums = lax.psum((gram_part, cross_part), FEAT_AXES)]
    pallas_call x0 -> x1, Pallas kernels: none -> 103 us  [solve(): pl.pallas_call(functools.partial(solve_kernel, n, nq), out_shape=(jax.Sha...]
    all_to_all x3 -> x0, blocking collectives: 82.5 us -> none  [the longest x1 38.6 us: sent_and_summed(): blocks = lax.all_to_all(split_up(shard, dim, size), axis, 0, 0, tiled=True)]
    all_gather x2 -> x3, waiting for transfers between devices: 57.6 us -> 118 us  [the longest x1 118 us: on_device(): sums = lax.all_gather(sums, DP_FEAT, axis=0, tiled=True)]
    another operation x44 -> x0, matrix products: 47.6 us -> none  [the longest x14 25.9 us: on_device(): factor = jnp.linalg.cholesky(gram_matrix)]
    psum x4 -> x1, blocking collectives: 40.4 us -> 74.8 us  [on_device(): squares = lax.psum(squares.reshape(-1), FEAT_AXES + DP)]
  transfers between devices with their start and end apart: 3 -> 6, of which waited for: 3 -> 4; matrix products, arithmetic and copies ran while one was open for 0% -> 2% of each run, Pallas kernels for 0% -> 13%
where the time goes in v1:
time: 796 us; the launch traced here: 794 us
  waiting for transfers between devices  553 us (69%)
  Pallas kernels  103 us (13%)
  blocking collectives  74.8 us (9%)
  matrix products  28.3 us (4%)
  between operations  13.3 us (2%)
  starting transfers between devices  11.7 us (1%)
    reduce_scatter x1, waiting for transfers between devices, on_device(): lax.psum_scatter(partial_value, FEAT_AXES, scatter_dimension=0, tiled=True)  214 us
    reduce_scatter x1, waiting for transfers between devices, on_device(): sums = lax.psum_scatter(sums, FEAT_AXES, scatter_dimension=0, tiled=True)  203 us
    all_gather x1, waiting for transfers between devices, on_device(): sums = lax.all_gather(sums, DP_FEAT, axis=0, tiled=True)  118 us
    pallas_call x1, Pallas kernels, solve(): pl.pallas_call(functools.partial(solve_kernel, n, nq), out_shape=(jax.Sha...  103 us
    psum x1, blocking collectives, on_device(): squares = lax.psum(squares.reshape(-1), FEAT_AXES + DP)  74.8 us
    dot_general x7, matrix products, contract_last(): lax.dot_general(left, right, (((1,), (1,)), ((), ())), preferred_element_...  28.3 us
    all_to_all x1, waiting for transfers between devices, on_device(): lax.all_to_all(query_grads, FEAT_AXES, split_axis=1, concat_axis=0, tiled...  16.8 us
  transfers between devices with their start and end apart: 6, of which 4 were waited for; matrix products, arithmetic and copies ran while one was open for 2% of the time, Pallas kernels for 13%

profile of v1, /device:TPU:32, one launch (start us, length us, event | category | flops | bytes accessed | tf_op | source)
XLA Modules:
  0.0 793.8 jit_solution(12298994837143729673)
XLA Ops:
  6.5 0.0 copy-start.3
  6.5 0.0 copy-start.1
  6.5 0.0 all-gather.4.cloned.1.call-start
  6.5 0.7 all-gather.4.cloned.1.call-update
  7.3 11.4 %all-to-all-start = ((bf16[2,32,4096]{2,0,1:T(2,128)(2,1)}), bf16[2,32,4096]{2,0,1:T(2,128)(2,1)S(1)}, u32[]{:S(2)}, u32[]{:S(2)}) async-start(bf16[2,32,4096]{2,0,1:T(2,128)(2,1)} %bitcast.23), calls=%async_computation | async-start | bytes 1048576 | tf_op jit(solution)/shard_map/all_to_all | solution.py:173
  18.6 0.0 reduce-scatter.5.cloned.1.call-start
  18.7 0.0 copy-done.3
  18.7 0.8 and_reduce_fusion
  19.5 16.8 %all-to-all-done = bf16[2,32,4096]{2,0,1:T(2,128)(2,1)S(1)} async-done(((bf16[2,32,4096]{2,0,1:T(2,128)(2,1)}), bf16[2,32,4096]{2,0,1:T(2,128)(2,1)S(1)}, u32[]{:S(2)}, u32[]{:S(2)}) %all-to-all-start) | async-done | bytes 524320 | tf_op jit(solution)/shard_map/all_to_all | solution.py:173
  36.3 0.6 multiply_reduce_fusion
  36.9 0.6 broadcast_select_fusion
  37.5 0.1 reshape.51
  37.7 0.1 reshape.52
  37.7 0.2 all_to_all.17
  37.9 0.0 copy-start
  38.0 74.8 %psum.7 = f32[512]{0:T(512)S(1)} all-reduce(f32[512]{0:T(512)S(1)} %reshape.52), channel_id=1, replica_groups=mesh['feat_0'=4,'feat_1'=8,'dp_0'=4,'dp_1'=2] {'feat_0','feat_1','dp_0',..., use_global_device_ids=true, to_apply=%region_2.0 | all-reduce | flops 512 | bytes 4096 | tf_op jit(solution)/shard_map/psum | solution.py:180
  112.8 0.0 copy-done.1
  112.8 1.3 pad_maximum_fusion.1
  114.1 0.0 copy-start.2
  114.1 0.0 all-gather.4.cloned.1.call-done
  114.1 3.0 fusion.1
  117.2 0.0 copy-done
  117.2 0.0 copy-done.2
  117.2 2.5 fusion.3
  119.7 2.5 fusion.5
  122.2 2.5 fusion.7
  124.7 1.0 pad_maximum_fusion.2
  125.7 0.0 reduce-scatter.5.cloned.1.call-update
  125.7 0.0 all-gather.6.cloned.1.call-start
  125.7 9.2 %reduce-precision_convert_fusion = (bf16[512,1024]{1,0:T(8,128)(2,1)S(1)}, bf16[512,1024]{1,0:T(8,128)(2,1)S(1)}) fusion(bf16[512,4096]{1,0:T(8,128)(2,1)} %param.7, bf16[1024,4096]{1,0:T(8,128)(2,1)} %all-gather.4.cloned.1.call-done), kind=kOutput, calls=%fused_computation.1 | convolution fusion | flops 4297064448 | bytes 14680064 | tf_op jit(solution)/shard_map/dot_general | solution.py:169
  134.9 0.1 pad_maximum_fusion
  135.1 203.1 %reduce-scatter.5.cloned.1.call-done = f32[24,256]{1,0:T(8,128)} async-done(((f32[768,256]{1,0:T(8,128)}), f32[24,256]{1,0:T(8,128)}) %reduce-scatter.5.cloned.1.call-update) | async-done | bytes 24592 | tf_op jit(solution)/shard_map/reduce_scatter | solution.py:184
  338.2 0.0 all-gather.6.cloned.1.call-update
  338.2 0.0 all-gather.8.cloned.1.call-start
  338.2 118.4 %all-gather.6.cloned.1.call-done = f32[6144,256]{1,0:T(8,128)} async-done(((f32[24,256]{1,0:T(8,128)}), f32[6144,256]{1,0:T(8,128)}) %all-gather.6.cloned.1.call-update) | async-done | bytes 6291472 | tf_op jit(solution)/shard_map/all_gather | solution.py:190
  456.7 0.0 all-gather.8.cloned.1.call-update
  456.7 0.2 reduce-scatter.7.cloned.1.call-start
  456.9 103.2 %solve.1 = (bf16[512,1024]{1,0:T(8,128)(2,1)}, f32[512,128]{1,0:T(8,128)}, f32[8,128]{1,0:T(8,128)}) custom-call(f32[8,4,192,256]{3,2,1,0:T(8,128)} %bitcast.24), custom_call_target="tpu_custom_call" | custom-call | flops 20000000000 | bytes 8000000 | tf_op jit(solution)/shard_map/solve/pallas_call | solution.py:147
  560.1 1.2 slice.36
  561.3 1.1 slice_reduce_fusion
  562.3 0.6 multiply_divide_fusion
  562.9 2.8 fusion.9
  565.8 0.0 all-gather.8.cloned.1.call-done
  565.8 5.8 fusion.14
  571.6 1.3 copy.14
  572.9 0.0 reduce-scatter.7.cloned.1.call-update
  573.0 214.3 %reduce-scatter.7.cloned.1.call-done = f32[16,512]{1,0:T(8,128)} async-done(((f32[512,512]{1,0:T(8,128)}), f32[16,512]{1,0:T(8,128)}) %reduce-scatter.7.cloned.1.call-update) | async-done | bytes 32784 | tf_op jit(solution)/shard_map/reduce_scatter | solution.py:200
  (2 shorter events, 0.0 us)
Async XLA Ops:
  6.5 12.2 %copy-start.3 = (s32[2]{0:T(128)S(1)}, s32[2]{0:T(128)}, u32[]{:S(2)}) copy-start(s32[2]{0:T(128)} %constant.38.clone.1) | copy-start | bytes 28
  6.5 106.3 %copy-start.1 = (bf16[128,4096]{1,0:T(8,128)(2,1)S(1)}, bf16[128,4096]{1,0:T(8,128)(2,1)}, u32[]{:S(2)}) copy-start(bf16[128,4096]{1,0:T(8,128)(2,1)} %param.6) | copy-start | bytes 3145732
  6.5 107.6 %all-gather.4.cloned.1.call-start = ((), (), s32[]{:S(2)}) async-start(), calls=%async_computation.3 | async-start | bytes 9437184 | tf_op jit(solution)/shard_map/all_gather | solution.py:174
  7.3 29.0 %all-to-all-start = ((bf16[2,32,4096]{2,0,1:T(2,128)(2,1)}), bf16[2,32,4096]{2,0,1:T(2,128)(2,1)S(1)}, u32[]{:S(2)}, u32[]{:S(2)}) async-start(bf16[2,32,4096]{2,0,1:T(2,128)(2,1)} %bitcast.23), calls=%async_computation | async-start | bytes 1048576 | tf_op jit(solution)/shard_map/all_to_all | solution.py:173
  18.6 319.5 %reduce-scatter.5.cloned.1.call-start = ((), (), s32[]{:S(2)}) async-start(), calls=%async_computation.4 | async-start | bytes 811008 | tf_op jit(solution)/shard_map/reduce_scatter | solution.py:184
  37.9 79.2 %copy-start = (bf16[64,4096]{1,0:T(8,128)(2,1)}, bf16[64,4096]{1,0:T(8,128)(2,1)S(1)}, u32[]{:S(2)}) copy-start(bf16[64,4096]{1,0:T(8,128)(2,1)S(1)} %all_to_all.17) | copy-start | bytes 1572868
  114.1 3.1 copy-start.2
  125.7 331.0 %all-gather.6.cloned.1.call-start = ((), (), s32[]{:S(2)}) async-start(), calls=%async_computation.5 | async-start | bytes 6316032 | tf_op jit(solution)/shard_map/all_gather | solution.py:190
  338.2 227.6 %all-gather.8.cloned.1.call-start = ((), (), s32[]{:S(2)}) async-start(), calls=%async_computation.6 | async-start | bytes 4718592 | tf_op jit(solution)/shard_map/all_gather | solution.py:192
  456.7 330.6 %reduce-scatter.7.cloned.1.call-start = ((), (), s32[]{:S(2)}) async-start(), calls=%async_computation.7 | async-start | bytes 1081344 | tf_op jit(solution)/shard_map/reduce_scatter | solution.py:200
Sparse Core Ops, SparseCore 0:
  9.2 55.6 all-gather.3
  125.8 212.3 reduce-scatter.4
  342.0 114.6 all-gather.5
  458.4 33.5 all-gather.7
  573.1 214.1 reduce-scatter.6

commit v2 on v1

v2 whole, which is shorter than its diff:
```python
import functools
import jax, jax.numpy as jnp
from jax import lax
from jax.experimental import pallas as pl
from jax.experimental.pallas import tpu as pltpu

BLK = 128
FEAT = 131072
BF = jnp.bfloat16
F32 = jnp.float32

def split3(x):
    h = x.astype(BF)
    r = x - h.astype(F32)
    m = r.astype(BF)
    l = (r - m.astype(F32)).astype(BF)
    return h, m, l

def cat_left(x):
    h, m, l = split3(x)
    return jnp.concatenate([h, h, m, h, l, m], axis=1)

def cat_right(x):
    h, m, l = split3(x)
    return jnp.concatenate([h, m, h, l, h, m], axis=0)

def mm(a, b):
    return jnp.dot(a, b, preferred_element_type=F32)

def put_rows(x, j, row0, row1):
    g = j // 8 * 8
    sub = lax.broadcasted_iota(jnp.int32, (8, x.shape[1]), 0)
    block = jnp.where(sub == j - g, row0, jnp.where(sub == j - g + 1, row1, x[g:g+8]))
    parts = ([x[:g]] if g else []) + [block] + ([x[g+8:]] if g + 8 < x.shape[0] else [])
    return jnp.concatenate(parts, axis=0)

def sweep(p, off):
    rows = p.shape[0]
    lane = lax.broadcasted_iota(jnp.int32, (1, p.shape[1]), 1)
    def spread(x, i):
        return jnp.broadcast_to(x[:, i:i+1], x.shape)
    c0, c1 = spread(p, off), spread(p, off + 1)
    for j in range(0, rows, 2):
        e, f, h = c0[j:j+1], c0[j+1:j+2], c1[j+1:j+2]
        inv = 1.0 / (e * h - f * f)
        i00, i01, i11 = h * inv, -f * inv, e * inv
        more = j + 2 < rows
        if more:
            d0, d1 = spread(p, off + j + 2), spread(p, off + j + 3)
            x0, x1 = c0[j+2:j+3], c1[j+2:j+3]
            y0, y1 = c0[j+3:j+4], c1[j+3:j+4]
            u0, u1 = i00 * x0 + i01 * x1, i01 * x0 + i11 * x1
            v0, v1 = i00 * y0 + i01 * y1, i01 * y0 + i11 * y1
            n0 = put_rows(d0 - c0 * u0 - c1 * u1, j, u0, u1)
            n1 = put_rows(d1 - c0 * v0 - c1 * v1, j, v0, v1)
        first, second = lane == off + j, lane == off + j + 1
        r0 = jnp.where(first, 1.0, jnp.where(second, 0.0, p[j:j+1]))
        r1 = jnp.where(first, 0.0, jnp.where(second, 1.0, p[j+1:j+2]))
        t0 = i00 * r0 + i01 * r1
        t1 = i01 * r0 + i11 * r1
        p = put_rows(jnp.where(first | second, 0.0, p) - c0 * t0 - c1 * t1, j, t0, t1)
        if more:
            c0, c1 = n0, n1
    return p

def inverse(a):
    n = a.shape[0]
    h = n // 2
    left = lax.broadcasted_iota(jnp.int32, (1, n), 1) < h
    top = sweep(a[:h], 0)
    low = jnp.where(left, 0.0, a[h:]) - mm(cat_left(a[h:, :h]), cat_right(top))
    low = sweep(low, h)
    high = jnp.where(left, top, 0.0) - mm(cat_left(top[:, h:]), cat_right(low))
    return jnp.concatenate([high, low], axis=0)

def across(a, b):
    return lax.dot_general(a, b, (((1,), (1,)), ((), ())), preferred_element_type=F32)

def solve_kernel(n, nq, m_ref, sb_ref, sq_ref, out_ref, a, t, dinv, w, lc, w2):
    g = n // BLK
    qs = nq // g
    rows = BLK + qs
    chunks = n // 256
    tot = jnp.zeros((BLK, BLK), F32)
    eye = (lax.broadcasted_iota(jnp.int32, (BLK, BLK), 0) == lax.broadcasted_iota(jnp.int32, (BLK, BLK), 1)).astype(F32)
    for k in range(g):
        for c in range(chunks):
            a[k*BLK:(k+1)*BLK, c*256:(c+1)*256] = m_ref[k, c*rows:c*rows+BLK, :]
            t[k*qs:(k+1)*qs, c*256:(c+1)*256] = m_ref[k, c*rows+BLK:(c+1)*rows, :]
        tot = tot + a[k*BLK:(k+1)*BLK, k*BLK:(k+1)*BLK] * eye
    trace = jnp.sum(jnp.sum(tot, axis=1, keepdims=True), axis=0, keepdims=True)
    damping = 0.1 * trace / (n * FEAT) + 1e-06
    for k in range(g):
        s = slice(k*BLK, (k+1)*BLK)
        a[s, s] = a[s, s] + eye * (n * damping)
    tiles = n // 256

    def update(ref, rt, ct):
        rs = pl.ds(pl.multiple_of(rt * 256, 256), 256)
        cs = pl.ds(pl.multiple_of(ct * 256, 256), 256)
        ref[rs, cs] = ref[rs, cs] - mm(lc[rs, :], w[:, cs])

    def set_left(ref, rt, ks):
        rs = pl.ds(pl.multiple_of(rt * 256, 256), 256)
        lc[rs, :] = cat_left(ref[rs, ks])

    col = lax.broadcasted_iota(jnp.int32, (1, n), 1)

    def forward(k, _):
        ks = pl.ds(pl.multiple_of(k * BLK, BLK), BLK)
        d = inverse(a[ks, ks])
        dinv[ks, :] = d
        lo = (k + 1) // 2
        dl = cat_left(d)
        def make_w(ct, _):
            cs = pl.ds(pl.multiple_of(ct * 256, 256), 256)
            cc = lax.broadcasted_iota(jnp.int32, (1, 256), 1) + ct * 256
            v = mm(dl, cat_right(a[ks, cs]))
            w[:, cs] = cat_right(jnp.where(cc >= (k + 1) * BLK, v, 0.0))
            return 0
        lax.fori_loop(lo, tiles, make_w, 0)
        def rows_a(rt, _):
            set_left(a, rt, ks)
            def cols(ct, _):
                update(a, rt, ct)
                return 0
            return lax.fori_loop(lo, tiles, cols, 0)
        lax.fori_loop(lo, tiles, rows_a, 0)
        def rows_t(rt, _):
            set_left(t, rt, ks)
            def cols(ct, _):
                update(t, rt, ct)
                return 0
            return lax.fori_loop(lo, tiles, cols, 0)
        lax.fori_loop(0, nq // 256, rows_t, 0)
        return 0
    lax.fori_loop(0, g, forward, 0)

    def backward(i, _):
        k = g - 1 - i
        ks = pl.ds(pl.multiple_of(k * BLK, BLK), BLK)
        dr = cat_right(dinv[ks, :])
        hi = (k + 1) // 2
        def make_w(ct, _):
            cs = pl.ds(pl.multiple_of(ct * 256, 256), 256)
            cc = lax.broadcasted_iota(jnp.int32, (1, 256), 1) + ct * 256
            w[:, cs] = cat_right(jnp.where(cc < k * BLK, a[ks, cs], 0.0))
            return 0
        lax.fori_loop(0, hi, make_w, 0)
        def rows_t(rt, _):
            rs = pl.ds(pl.multiple_of(rt * 256, 256), 256)
            x = mm(cat_left(t[rs, ks]), dr)
            t[rs, ks] = x
            lc[rs, :] = cat_left(x)
            def cols(ct, _):
                update(t, rt, ct)
                return 0
            return lax.fori_loop(0, hi, cols, 0)
        lax.fori_loop(0, nq // 256, rows_t, 0)
        return 0
    lax.fori_loop(0, g, backward, 0)
    ones = jnp.ones((8, 768), BF)
    squares = jnp.zeros((8, 256), F32)
    for k in range(g):
        squares = squares + m_ref[k, chunks*rows:chunks*rows+8, :]
    scales = []
    for h in range(nq // 256):
        accs = []
        for k in range(h * 256 // qs, (h + 1) * 256 // qs):
            acc = jnp.zeros((qs, 256), F32)
            for c in range(chunks):
                x = t[k*qs:(k+1)*qs, c*256:(c+1)*256].astype(BF)
                w2[k*qs:(k+1)*qs, c*256:(c+1)*256] = x
                acc = acc + x.astype(F32) * m_ref[k, c*rows+BLK:(c+1)*rows, :]
            accs.append(acc)
        parts = split3(jnp.concatenate(accs, axis=0))
        dots = across(ones, jnp.concatenate(parts, axis=1))[:1]
        self_score = (squares[h:h+1] - dots) / damping
        scales.append(1.0 / (damping * jnp.sqrt(self_score)))
    def finish(rt, _):
        rs = pl.ds(pl.multiple_of(rt * 128, 128), 128)
        wide = sb_ref[rs, :]
        high = wide.astype(BF)
        low = (wide - high.astype(F32)).astype(BF)
        for h in range(nq // 256):
            hs = slice(h * 256, (h + 1) * 256)
            removed = across(high, w2[hs, :]) + across(low, w2[hs, :])
            out_ref[rs, hs] = ((sq_ref[rs, hs] - removed) * scales[h]).astype(BF)
        return 0
    lax.fori_loop(0, sb_ref.shape[0] // 128, finish, 0)

def solve(m, sb, sq):
    g = m.shape[0]
    ns, n = sb.shape
    nq = sq.shape[1]
    vm = pl.BlockSpec(memory_space=pltpu.VMEM)
    return pl.pallas_call(
        functools.partial(solve_kernel, n, nq),
        out_shape=jax.ShapeDtypeStruct((ns, nq), BF),
        in_specs=[vm] * 3, out_specs=vm,
        scratch_shapes=[pltpu.VMEM((n, n), F32), pltpu.VMEM((nq, n), F32), pltpu.VMEM((n, BLK), F32),
                        pltpu.VMEM((6*BLK, n), BF), pltpu.VMEM((max(n, nq), 6*BLK), BF), pltpu.VMEM((nq, n), BF)],
        compiler_params=pltpu.CompilerParams(vmem_limit_bytes=48 * 1024 * 1024),
        cost_estimate=pl.CostEstimate(flops=20_000_000_000, bytes_accessed=12_000_000, transcendentals=0),
        name="solve",
    )(m, sb, sq)


from jax.sharding import Mesh
from jax.sharding import PartitionSpec as P

FEAT_AXES = ("feat_0", "feat_1")
DP = ("dp_0", "dp_1")
DP_FEAT = ("dp_0", "dp_1", "feat_0", "feat_1")


def exchange(x):
    return lax.all_to_all(x, FEAT_AXES, 0, 0, tiled=True)


def on_device(query_grads, build_grads, scored_grads):
    q_local = lax.all_to_all(query_grads, FEAT_AXES, split_axis=1, concat_axis=0, tiled=True)
    build_all = lax.all_gather(build_grads, DP, axis=0, tiled=True)
    build_rows = build_all.shape[0]
    query_wide = q_local.astype(F32)
    squares = jnp.sum(query_wide * query_wide, axis=1)
    for axis in FEAT_AXES:
        squares = lax.psum(squares, axis)
    per_row = 256 // squares.shape[0]
    slot = lax.axis_index(DP)
    squares = lax.dynamic_update_slice(
        jnp.zeros((8, 256), F32), squares[None], (slot // per_row, slot % per_row * squares.shape[0])
    )
    rows = jnp.concatenate([build_grads, q_local], axis=0)
    squares, rows = lax.optimization_barrier((squares, rows))
    sums = jnp.concatenate([across(rows, build_all[c:c + 256]) for c in range(0, build_rows, 256)], axis=0)
    size = lax.axis_size(FEAT_AXES)
    sums = jnp.sum(exchange(sums.reshape(size, -1, 256)), axis=0)
    sums = exchange(jnp.broadcast_to(sums[None], (size, *sums.shape)))
    sums = jnp.concatenate([sums.reshape(-1, 256), squares], axis=0)
    sums = lax.all_gather(sums, DP, axis=0, tiled=True)
    query_all = lax.all_gather(q_local, DP, axis=0, tiled=True)
    score_query = across(scored_grads, query_all)
    score_build = across(scored_grads, build_all)
    sums, score_query, score_build = lax.optimization_barrier((sums, score_query, score_build))
    partial_value = solve(sums.reshape(build_rows // BLK, -1, 256), score_build, score_query)
    partial_value = exchange(partial_value.reshape(size, -1, partial_value.shape[1]))
    return jnp.sum(partial_value.astype(F32), axis=0)


def solution(mesh):
    torus = Mesh(mesh.devices.reshape(4, 8, 4, 2), ("feat_0", "feat_1", "dp_0", "dp_1"))
    in_specs = (P(DP_FEAT, None), P(DP, FEAT_AXES), P(DP, FEAT_AXES))
    out_specs = P(DP_FEAT, None)
    return jax.shard_map(
        on_device, mesh=torus, in_specs=in_specs, out_specs=out_specs, check_vma=False
    )
```

time: 796 us -> 286 us (0.36)
  waiting for transfers between devices: 553 us -> 28.1 us
  blocking collectives: 74.8 us -> 141 us
  Pallas kernels: 103 us -> 78.3 us
  starting transfers between devices: 11.7 us -> 0.08 us
    reduce_scatter x2 -> x0, waiting for transfers between devices: 417 us -> none  [the longest x1 214 us: on_device(): lax.psum_scatter(partial_value, FEAT_AXES, scatter_dimension=0, tiled=True)]
    all_to_all x0 -> x4, blocking collectives: none -> 118 us  [the longest x3 88.9 us: exchange(): return lax.all_to_all(x, FEAT_AXES, 0, 0, tiled=True)]
    all_gather x1, waiting for transfers between devices: 118 us -> 25.5 us  [on_device(): sums = lax.all_gather(sums, DP, axis=0, tiled=True)]
    psum x1 -> x2, blocking collectives: 74.8 us -> 22.7 us  [on_device(): squares = lax.psum(squares, axis)]
    pallas_call x1, Pallas kernels: 103 us -> 78.3 us  [solve(): pl.pallas_call(functools.partial(solve_kernel, n, nq), out_shape=jax.Shap...]
    all_to_all x1 -> x0, waiting for transfers between devices: 16.8 us -> none  [on_device(): lax.all_to_all(query_grads, FEAT_AXES, split_axis=1, concat_axis=0, tiled...]
    all_to_all x1 -> x0, starting transfers between devices: 11.4 us -> none  [on_device(): lax.all_to_all(query_grads, FEAT_AXES, split_axis=1, concat_axis=0, tiled...]
    dot_general x7 -> x6, matrix products: 28.3 us -> 20.4 us  [across(): lax.dot_general(a, b, (((1,), (1,)), ((), ())), preferred_element_type=F32)]
  transfers between devices with their start and end apart: 6 -> 3, of which waited for: 4 -> 2; matrix products, arithmetic and copies ran while one was open for 2% -> 8% of each run, Pallas kernels for 13% -> 0%
where the time goes in v2:
time: 286 us
  blocking collectives  141 us (49%)
  Pallas kernels  78.3 us (27%)
  waiting for transfers between devices  28.1 us (10%)
  matrix products  20.4 us (7%)
  between operations  13.3 us (5%)
  other arithmetic  3.54 us (1%)
    all_to_all x3, blocking collectives, exchange(): return lax.all_to_all(x, FEAT_AXES, 0, 0, tiled=True)  88.9 us
    pallas_call x1, Pallas kernels, solve(): pl.pallas_call(functools.partial(solve_kernel, n, nq), out_shape=jax.Shap...  78.3 us
    all_to_all x1, blocking collectives, on_device(): lax.all_to_all(query_grads, FEAT_AXES, split_axis=1, concat_axis=0, tiled...  29 us
    all_gather x1, waiting for transfers between devices, on_device(): sums = lax.all_gather(sums, DP, axis=0, tiled=True)  25.5 us
    psum x2, blocking collectives, on_device(): squares = lax.psum(squares, axis)  22.7 us
    dot_general x6, matrix products, across(): lax.dot_general(a, b, (((1,), (1,)), ((), ())), preferred_element_type=F32)  20.4 us
  transfers between devices with their start and end apart: 3, of which 2 were waited for; matrix products, arithmetic and copies ran while one was open for 8% of the time, Pallas kernels for 0%

profile of v2, /device:TPU:32, one launch (start us, length us, event | category | flops | bytes accessed | tf_op | source)
XLA Modules:
  0.0 285.7 jit_solution(9953838113337153960)
XLA Ops:
  6.5 0.0 copy-start
  6.5 0.0 all-gather.4.cloned.1.call-start
  6.5 0.7 all-gather.4.cloned.1.call-update
  7.3 0.0 all-gather.8.cloned.1.call-start
  7.3 29.0 %all_to_all.34 = bf16[2,32,4096]{2,0,1:T(2,128)(2,1)S(1)} all-to-all(bf16[2,32,4096]{2,0,1:T(2,128)(2,1)} %bitcast.20), channel_id=1, replica_groups=mesh['feat_0'=4,'feat_1'=8,'dp_0'=4,'dp_1'=2] {'feat_0','feat_1'}, dimensions={1} | all-to-all | bytes 1048576 | tf_op jit(solution)/shard_map/all_to_all | solution.py:222
  36.3 1.0 all_to_all.26
  37.3 0.0 all-gather.8.cloned.1.call-update
  37.3 0.0 all-gather.6.cloned.1.call-start
  37.4 0.6 multiply_reduce_fusion
  38.0 0.1 reduce_sum.30
  38.1 8.9 %psum.14 = f32[64]{0:T(128)S(1)} all-reduce(f32[64]{0:T(128)S(1)} %reduce_sum.30), channel_id=1, replica_groups=mesh['feat_0'=4,'feat_1'=8,'dp_0'=4,'dp_1'=2] {'feat_0'}, use_global_device_ids=true, to_apply=%region_1.0 | all-reduce | flops 64 | bytes 512 | tf_op jit(solution)/shard_map/psum | solution.py:228
  47.0 13.8 %psum.15 = f32[1,64]{1,0:T(1,128)S(1)} all-reduce(f32[1,64]{1,0:T(1,128)S(1)} %bitcast.22), channel_id=1, replica_groups=mesh['feat_0'=4,'feat_1'=8,'dp_0'=4,'dp_1'=2] {'feat_1'}, use_global_device_ids=true, to_apply=%region_2.0 | all-reduce | flops 64 | bytes 512 | tf_op jit(solution)/shard_map/psum | solution.py:228
  60.8 0.2 dynamic_update_slice.3
  61.1 0.0 copy-done
  61.1 1.1 pad_maximum_fusion
  62.2 1.8 all-gather.4.cloned.1.call-done
  64.0 0.0 copy-start.1
  64.0 2.6 fusion
  66.6 2.9 %fusion.2 = f32[192,256]{1,0:T(8,128)S(1)} fusion(bf16[192,4096]{1,0:T(8,128)(2,1)S(1)} %pad_maximum_fusion, bf16[1024,4096]{1,0:T(8,128)(2,1)} %all-gather.4.cloned.1.call-done), kind=kOutput, calls=%fused_computation.2 | convolution fusion | flops 402653184 | bytes 3866624 | tf_op jit(solution)/shard_map/dot_general | solution.py:77
  69.5 0.0 copy-done.1
  69.5 0.8 fusion.4
  70.3 0.8 fusion.6
  71.2 0.1 pad_maximum_fusion.2
  71.2 33.3 %all_to_all.35 = f32[32,24,256]{2,1,0:T(8,128)S(1)} all-to-all(f32[32,24,256]{2,1,0:T(8,128)S(1)} %bitcast.18), channel_id=1, replica_groups=mesh['feat_0'=4,'feat_1'=8,'dp_0'=4,'dp_1'=2] {'feat_0','feat_1'}, dimensions={0} | all-to-all | bytes 1572864 | tf_op jit(solution)/shard_map/all_to_all | solution.py:218
  104.5 0.1 reduce_sum.31
  104.6 0.1 broadcast_in_dim.14
  104.6 27.7 %all_to_all.36 = f32[32,24,256]{2,1,0:T(8,128)S(1)} all-to-all(f32[32,24,256]{2,1,0:T(8,128)S(1)} %broadcast_in_dim.14), channel_id=1, replica_groups=mesh['feat_0'=4,'feat_1'=8,'dp_0'=4,'dp_1'=2] {'feat_0','feat_1'}, dimensions={0} | all-to-all | bytes 1572864 | tf_op jit(solution)/shard_map/all_to_all | solution.py:218
  132.3 1.0 pad_maximum_fusion.1
  133.3 0.0 all-gather.6.cloned.1.call-update
  133.3 0.0 all-gather.8.cloned.1.call-done
  133.4 0.0 copy-start.2
  133.4 6.0 %fusion.8.sq_ref = f32[512,512]{1,0:T(8,128)S(1)} fusion(bf16[512,4096]{1,0:T(8,128)(2,1)} %param.5, bf16[512,4096]{1,0:T(8,128)(2,1)} %all-gather.8.cloned.1.call-done), kind=kOutput, calls=%fused_computation.13 | convolution fusion | flops 2147483648 | bytes 9437184 | tf_op jit(solution)/shard_map/dot_general | solution.py:77
  139.3 0.0 copy-done.2
  139.3 7.3 %fusion.9.sb_ref = f32[512,1024]{1,0:T(8,128)S(1)} fusion(bf16[512,4096]{1,0:T(8,128)(2,1)S(1)} %copy-done.2, bf16[1024,4096]{1,0:T(8,128)(2,1)} %all-gather.4.cloned.1.call-done), kind=kOutput, calls=%fused_computation.14 | convolution fusion | flops 4294967296 | bytes 14680064 | tf_op jit(solution)/shard_map/dot_general | solution.py:77
  146.7 25.5 %all-gather.6.cloned.1.call-done = f32[6208,256]{1,0:T(8,128)} async-done(((f32[776,256]{1,0:T(8,128)}), f32[6208,256]{1,0:T(8,128)}) %all-gather.6.cloned.1.call-update) | async-done | bytes 6357008 | tf_op jit(solution)/shard_map/all_gather | solution.py:241
  172.2 78.3 %solve.1 = bf16[512,512]{1,0:T(8,128)(2,1)S(1)} custom-call(f32[8,776,256]{2,1,0:T(8,128)} %bitcast.21, f32[512,1024]{1,0:T(8,128)S(1)} %fusion.9.sb_ref, f32[512,512]{1,0:T(8,128)S(1)} %fusion.8.sq_ref), custom_call_target="tpu_custom_call" | custom-call | flops 20000000000 | bytes 12000000 | tf_op jit(solution)/shard_map/solve/pallas_call | solution.py:197
  250.5 27.9 %all_to_all.37 = bf16[32,16,512]{2,1,0:T(8,128)(2,1)S(1)} all-to-all(bf16[32,16,512]{2,1,0:T(8,128)(2,1)S(1)} %bitcast.16), channel_id=1, replica_groups=mesh['feat_0'=4,'feat_1'=8,'dp_0'=4,'dp_1'=2] {'feat_0','feat_1'}, dimensions={0} | all-to-all | bytes 1048576 | tf_op jit(solution)/shard_map/all_to_all | solution.py:218
  278.4 0.7 convert_reduce_fusion
  (1 shorter events, 0.0 us)
Async XLA Ops:
  6.5 54.5 %copy-start = (bf16[128,4096]{1,0:T(8,128)(2,1)S(1)}, bf16[128,4096]{1,0:T(8,128)(2,1)}, u32[]{:S(2)}) copy-start(bf16[128,4096]{1,0:T(8,128)(2,1)} %param.4) | copy-start | bytes 3145732
  6.5 57.5 %all-gather.4.cloned.1.call-start = ((), (), s32[]{:S(2)}) async-start(), calls=%async_computation.4 | async-start | bytes 9437184 | tf_op jit(solution)/shard_map/all_gather | solution.py:223
  7.3 126.1 %all-gather.8.cloned.1.call-start = ((), (), s32[]{:S(2)}) async-start(), calls=%async_computation.6 | async-start | bytes 4718592 | tf_op jit(solution)/shard_map/all_gather | solution.py:242
  37.3 134.9 %all-gather.6.cloned.1.call-start = ((), (), s32[]{:S(2)}) async-start(), calls=%async_computation.5 | async-start | bytes 7151616 | tf_op jit(solution)/shard_map/all_gather | solution.py:241
  64.0 5.5 %copy-start.1 = (bf16[1024,4096]{1,0:T(8,128)(2,1)S(1)}, bf16[1024,4096]{1,0:T(8,128)(2,1)}, u32[]{:S(2)}) copy-start(bf16[1024,4096]{1,0:T(8,128)(2,1)} %all-gather.4.cloned.1.call-done) | copy-start | bytes 25165828
  133.4 6.0 %copy-start.2 = (bf16[512,4096]{1,0:T(8,128)(2,1)S(1)}, bf16[512,4096]{1,0:T(8,128)(2,1)}, u32[]{:S(2)}) copy-start(bf16[512,4096]{1,0:T(8,128)(2,1)} %param.5) | copy-start | bytes 12582916
Sparse Core Ops, SparseCore 0:
  9.2 54.7 all-gather.3
  65.9 34.7 all-gather.7
  133.4 38.6 all-gather.5

commit v3 on v2

v3 whole, which is shorter than its diff:
```python
import functools
import jax, jax.numpy as jnp
from jax import lax
from jax.experimental import pallas as pl
from jax.experimental.pallas import tpu as pltpu

BLK = 128
FEAT = 131072
BF = jnp.bfloat16
F32 = jnp.float32

def split3(x):
    h = x.astype(BF)
    r = x - h.astype(F32)
    m = r.astype(BF)
    l = (r - m.astype(F32)).astype(BF)
    return h, m, l

def split2(x):
    h = x.astype(BF)
    return h, (x - h.astype(F32)).astype(BF)

def left6(x):
    h, m, l = split3(x)
    return jnp.concatenate([h, h, m, m, h, l], axis=1)

def right6(x):
    h, m, l = split3(x)
    return jnp.concatenate([h, m, h, m, l, h], axis=0)

def left4(x):
    h, m = split2(x)
    return jnp.concatenate([h, h, m, m], axis=1)

def mixed4(x):
    h, m = split2(x)
    return jnp.concatenate([h, m, h, m], axis=1)

def mm(a, b):
    return jnp.dot(a, b, preferred_element_type=F32)

def across(a, b):
    return lax.dot_general(a, b, (((1,), (1,)), ((), ())), preferred_element_type=F32)

def put_rows(x, j, row0, row1):
    g = j // 8 * 8
    sub = lax.broadcasted_iota(jnp.int32, (8, x.shape[1]), 0)
    block = jnp.where(sub == j - g, row0, jnp.where(sub == j - g + 1, row1, x[g:g+8]))
    parts = ([x[:g]] if g else []) + [block] + ([x[g+8:]] if g + 8 < x.shape[0] else [])
    return jnp.concatenate(parts, axis=0)

def sweep(p, off, tick):
    rows = p.shape[0]
    lane = lax.broadcasted_iota(jnp.int32, (1, p.shape[1]), 1)
    def spread(x, i):
        return jnp.broadcast_to(x[:, i:i+1], x.shape)
    c0, c1 = spread(p, off), spread(p, off + 1)
    for j in range(0, rows, 2):
        e, f, h = c0[j:j+1], c0[j+1:j+2], c1[j+1:j+2]
        inv = 1.0 / (e * h - f * f)
        i00, i01, i11 = h * inv, -f * inv, e * inv
        more = j + 2 < rows
        if more:
            d0, d1 = spread(p, off + j + 2), spread(p, off + j + 3)
            x0, x1 = c0[j+2:j+3], c1[j+2:j+3]
            y0, y1 = c0[j+3:j+4], c1[j+3:j+4]
            u0, u1 = i00 * x0 + i01 * x1, i01 * x0 + i11 * x1
            v0, v1 = i00 * y0 + i01 * y1, i01 * y0 + i11 * y1
            n0 = put_rows(d0 - c0 * u0 - c1 * u1, j, u0, u1)
            n1 = put_rows(d1 - c0 * v0 - c1 * v1, j, v0, v1)
        first, second = lane == off + j, lane == off + j + 1
        r0 = jnp.where(first, 1.0, jnp.where(second, 0.0, p[j:j+1]))
        r1 = jnp.where(first, 0.0, jnp.where(second, 1.0, p[j+1:j+2]))
        t0 = i00 * r0 + i01 * r1
        t1 = i01 * r0 + i11 * r1
        p = put_rows(jnp.where(first | second, 0.0, p) - c0 * t0 - c1 * t1, j, t0, t1)
        if more:
            c0, c1 = n0, n1
        tick()
    return p

def inverse(a, tick):
    n = a.shape[0]
    h = n // 2
    left = lax.broadcasted_iota(jnp.int32, (1, n), 1) < h
    top = sweep(a[:h], 0, tick)
    low = jnp.where(left, 0.0, a[h:]) - mm(left6(a[h:, :h]), right6(top))
    low = sweep(low, h, tick)
    high = jnp.where(left, top, 0.0) - mm(left6(top[:, h:]), right6(low))
    return jnp.concatenate([high, low], axis=0)

TILE = 256

class Spread:
    def __init__(self, tasks, steps):
        self.tasks, self.steps, self.step, self.done = tasks, steps, 0, 0
    def __call__(self):
        self.step += 1
        upto = len(self.tasks) * self.step // self.steps
        while self.done < upto:
            self.tasks[self.done]()
            self.done += 1

def solve_kernel(n, nq, m_ref, sb_ref, sq_ref, out_ref, a, t, z, s, dinv, w, la, lt, lz, dq):
    g = n // BLK
    ns = sb_ref.shape[0]
    qs = nq // g
    rows = BLK + qs
    chunks = n // 256
    tiles = n // TILE
    tot = jnp.zeros((BLK, BLK), F32)
    eye = (lax.broadcasted_iota(jnp.int32, (BLK, BLK), 0) == lax.broadcasted_iota(jnp.int32, (BLK, BLK), 1)).astype(F32)
    for k in range(g):
        for c in range(chunks):
            a[k*BLK:(k+1)*BLK, c*256:(c+1)*256] = m_ref[k, c*rows:c*rows+BLK, :]
            t[k*qs:(k+1)*qs, c*256:(c+1)*256] = m_ref[k, c*rows+BLK:(c+1)*rows, :]
        tot = tot + a[k*BLK:(k+1)*BLK, k*BLK:(k+1)*BLK] * eye
    trace = jnp.sum(jnp.sum(tot, axis=1, keepdims=True), axis=0, keepdims=True)
    damping = 0.1 * trace / (n * FEAT) + 1e-06
    for k in range(g):
        d = slice(k*BLK, (k+1)*BLK)
        a[d, d] = a[d, d] + eye * (n * damping)
    z[...] = sb_ref[...]
    s[...] = sq_ref[...]
    dq[...] = jnp.zeros(dq.shape, F32)
    dinv[...] = inverse(a[:BLK, :BLK], lambda: None)

    def strip(i):
        return slice(i * TILE, (i + 1) * TILE)

    def score_tasks(ks, d):
        d4 = right6(d)[:4*BLK]
        def dots(rt):
            r = strip(rt)
            lt[r, :] = left4(t[r, ks])
            dq[r, :] = dq[r, :] + mm(lt[r, :], d4) * t[r, ks]
        def scores(rt):
            r = strip(rt)
            lz[r, :] = left4(z[r, ks])
            v = mixed4(mm(lz[r, :], d4))
            for ct in range(nq // TILE):
                c = strip(ct)
                s[r, c] = s[r, c] - across(v, lt[c, :])
        return [functools.partial(dots, i) for i in range(nq // TILE)] + [functools.partial(scores, i) for i in range(ns // TILE)]

    def forward(lo, k, _):
        ks = pl.ds(pl.multiple_of(k * BLK, BLK), BLK)
        ns_ = pl.ds(pl.multiple_of((k + 1) * BLK, BLK), BLK)
        d = dinv[...]
        dl = left6(d)
        near = mm(dl, right6(a[ks, ns_]))
        block = a[ns_, ns_] - mm(left6(a[ns_, ks]), right6(near))

        def make_w(ct):
            c = strip(ct)
            cc = lax.broadcasted_iota(jnp.int32, (1, TILE), 1) + ct * TILE
            w[:, c] = right6(jnp.where(cc >= (k + 1) * BLK, mm(dl, right6(a[ks, c])), 0.0))
        def make_la(rt):
            la[strip(rt), :] = left6(a[strip(rt), ks])
        def update(ref, left, terms, rt, ct):
            r, c = strip(rt), strip(ct)
            ref[r, c] = ref[r, c] - mm(left[r, :], w[:terms*BLK, c])
        tasks = [functools.partial(make_w, i) for i in range(lo, tiles)]
        tasks += [functools.partial(make_la, i) for i in range(lo, tiles)]
        tasks += score_tasks(ks, d)
        for ct in range(lo, tiles):
            tasks += [functools.partial(update, a, la, 6, rt, ct) for rt in range(lo, tiles)]
            tasks += [functools.partial(update, t, lt, 4, rt, ct) for rt in range(nq // TILE)]
            tasks += [functools.partial(update, z, lz, 4, rt, ct) for rt in range(ns // TILE)]
        tick = Spread(tasks, BLK // 2)
        dinv[...] = inverse(block, tick)
        return 0

    for first, last, lo in SECTIONS:
        lax.fori_loop(first, last, functools.partial(forward, lo), 0)
    for task in score_tasks(slice(n - BLK, n), dinv[...]):
        task()

    squares = jnp.zeros((8, 256), F32)
    for k in range(g):
        squares = squares + m_ref[k, chunks*rows:chunks*rows+8, :]
    ones = jnp.ones((8, 3 * BLK), BF)
    for h in range(nq // 256):
        c = strip(h)
        dots = across(ones, jnp.concatenate(split3(dq[c, :]), axis=1))[:1]
        self_score = (squares[h:h+1] - dots) / damping
        out_ref[:, c] = (s[:, c] * (1.0 / (damping * jnp.sqrt(self_score)))).astype(BF)

SECTIONS = ((0, 4, 0), (4, 7, 2))

def solve(m, sb, sq):
    g = m.shape[0]
    ns, n = sb.shape
    nq = sq.shape[1]
    vm = pl.BlockSpec(memory_space=pltpu.VMEM)
    return pl.pallas_call(
        functools.partial(solve_kernel, n, nq),
        out_shape=jax.ShapeDtypeStruct((ns, nq), BF),
        in_specs=[vm] * 3, out_specs=vm,
        scratch_shapes=[pltpu.VMEM((n, n), F32), pltpu.VMEM((nq, n), F32), pltpu.VMEM((ns, n), F32), pltpu.VMEM((ns, nq), F32),
                        pltpu.VMEM((BLK, BLK), F32), pltpu.VMEM((6*BLK, n), BF), pltpu.VMEM((n, 6*BLK), BF),
                        pltpu.VMEM((nq, 4*BLK), BF), pltpu.VMEM((ns, 4*BLK), BF), pltpu.VMEM((nq, BLK), F32)],
        compiler_params=pltpu.CompilerParams(vmem_limit_bytes=48 * 1024 * 1024),
        cost_estimate=pl.CostEstimate(flops=20_000_000_000, bytes_accessed=12_000_000, transcendentals=0),
        name="solve",
    )(m, sb, sq)


from jax.sharding import Mesh
from jax.sharding import PartitionSpec as P

FEAT_AXES = ("feat_0", "feat_1")
DP = ("dp_0", "dp_1")
DP_FEAT = ("dp_0", "dp_1", "feat_0", "feat_1")


def exchange(x):
    return lax.all_to_all(x, FEAT_AXES, 0, 0, tiled=True)


def on_device(query_grads, build_grads, scored_grads):
    q_local = lax.all_to_all(query_grads, FEAT_AXES, split_axis=1, concat_axis=0, tiled=True)
    build_all = lax.all_gather(build_grads, DP, axis=0, tiled=True)
    build_rows = build_all.shape[0]
    query_wide = q_local.astype(F32)
    squares = jnp.sum(query_wide * query_wide, axis=1)
    for axis in FEAT_AXES:
        squares = lax.psum(squares, axis)
    per_row = 256 // squares.shape[0]
    slot = lax.axis_index(DP)
    squares = lax.dynamic_update_slice(
        jnp.zeros((8, 256), F32), squares[None], (slot // per_row, slot % per_row * squares.shape[0])
    )
    rows = jnp.concatenate([build_grads, q_local], axis=0)
    squares, rows = lax.optimization_barrier((squares, rows))
    sums = jnp.concatenate([across(rows, build_all[c:c + 256]) for c in range(0, build_rows, 256)], axis=0)
    size = lax.axis_size(FEAT_AXES)
    sums = jnp.sum(exchange(sums.reshape(size, -1, 256)), axis=0)
    sums = exchange(jnp.broadcast_to(sums[None], (size, *sums.shape)))
    sums = jnp.concatenate([sums.reshape(-1, 256), squares], axis=0)
    sums = lax.all_gather(sums, DP, axis=0, tiled=True)
    query_all = lax.all_gather(q_local, DP, axis=0, tiled=True)
    score_query = across(scored_grads, query_all)
    score_build = across(scored_grads, build_all)
    sums, score_query, score_build = lax.optimization_barrier((sums, score_query, score_build))
    partial_value = solve(sums.reshape(build_rows // BLK, -1, 256), score_build, score_query)
    partial_value = exchange(partial_value.reshape(size, -1, partial_value.shape[1]))
    return jnp.sum(partial_value.astype(F32), axis=0)


def solution(mesh):
    torus = Mesh(mesh.devices.reshape(4, 8, 4, 2), ("feat_0", "feat_1", "dp_0", "dp_1"))
    in_specs = (P(DP_FEAT, None), P(DP, FEAT_AXES), P(DP, FEAT_AXES))
    out_specs = P(DP_FEAT, None)
    return jax.shard_map(
        on_device, mesh=torus, in_specs=in_specs, out_specs=out_specs, check_vma=False
    )
```

time: 286 us -> 250 us (0.87)
  Pallas kernels: 78.3 us -> 41.7 us
    pallas_call x1, Pallas kernels: 78.3 us -> 41.7 us  [solve(): pl.pallas_call(functools.partial(solve_kernel, n, nq), out_shape=jax.Shap...]
  transfers between devices with their start and end apart: 3 -> 3, of which waited for: 2 -> 2; matrix products, arithmetic and copies ran while one was open for 8% -> 9% of each run, Pallas kernels for 0% -> 0%
where the time goes in v3:
time: 250 us; the launch traced here: 249 us
  blocking collectives  141 us (56%)
  Pallas kernels  41.7 us (17%)
  waiting for transfers between devices  28.1 us (11%)
  matrix products  20.4 us (8%)
  between operations  13.3 us (5%)
  other arithmetic  3.54 us (1%)
    all_to_all x3, blocking collectives, exchange(): return lax.all_to_all(x, FEAT_AXES, 0, 0, tiled=True)  88.9 us
    pallas_call x1, Pallas kernels, solve(): pl.pallas_call(functools.partial(solve_kernel, n, nq), out_shape=jax.Shap...  41.7 us
    all_to_all x1, blocking collectives, on_device(): lax.all_to_all(query_grads, FEAT_AXES, split_axis=1, concat_axis=0, tiled...  29 us
    all_gather x1, waiting for transfers between devices, on_device(): sums = lax.all_gather(sums, DP, axis=0, tiled=True)  25.5 us
    psum x2, blocking collectives, on_device(): squares = lax.psum(squares, axis)  22.7 us
    dot_general x6, matrix products, across(): lax.dot_general(a, b, (((1,), (1,)), ((), ())), preferred_element_type=F32)  20.4 us
  transfers between devices with their start and end apart: 3, of which 2 were waited for; matrix products, arithmetic and copies ran while one was open for 9% of the time, Pallas kernels for 0%

profile of v3, /device:TPU:32, one launch (start us, length us, event | category | flops | bytes accessed | tf_op | source)
XLA Modules:
  0.0 249.1 jit_solution(12460034569935003004)
XLA Ops:
  6.5 0.0 copy-start
  6.5 0.0 all-gather.4.cloned.1.call-start
  6.5 0.7 all-gather.4.cloned.1.call-update
  7.3 0.0 all-gather.8.cloned.1.call-start
  7.3 29.0 %all_to_all.34 = bf16[2,32,4096]{2,0,1:T(2,128)(2,1)S(1)} all-to-all(bf16[2,32,4096]{2,0,1:T(2,128)(2,1)} %bitcast.20), channel_id=1, replica_groups=mesh['feat_0'=4,'feat_1'=8,'dp_0'=4,'dp_1'=2] {'feat_0','feat_1'}, dimensions={1} | all-to-all | bytes 1048576 | tf_op jit(solution)/shard_map/all_to_all | solution.py:222
  36.3 1.0 all_to_all.26
  37.3 0.0 all-gather.8.cloned.1.call-update
  37.3 0.0 all-gather.6.cloned.1.call-start
  37.4 0.6 multiply_reduce_fusion
  38.0 0.1 reduce_sum.30
  38.1 8.9 %psum.14 = f32[64]{0:T(128)S(1)} all-reduce(f32[64]{0:T(128)S(1)} %reduce_sum.30), channel_id=1, replica_groups=mesh['feat_0'=4,'feat_1'=8,'dp_0'=4,'dp_1'=2] {'feat_0'}, use_global_device_ids=true, to_apply=%region_1.0 | all-reduce | flops 64 | bytes 512 | tf_op jit(solution)/shard_map/psum | solution.py:228
  47.0 13.8 %psum.15 = f32[1,64]{1,0:T(1,128)S(1)} all-reduce(f32[1,64]{1,0:T(1,128)S(1)} %bitcast.22), channel_id=1, replica_groups=mesh['feat_0'=4,'feat_1'=8,'dp_0'=4,'dp_1'=2] {'feat_1'}, use_global_device_ids=true, to_apply=%region_2.0 | all-reduce | flops 64 | bytes 512 | tf_op jit(solution)/shard_map/psum | solution.py:228
  60.8 0.2 dynamic_update_slice.3
  61.1 0.0 copy-done
  61.1 1.1 pad_maximum_fusion
  62.2 1.8 all-gather.4.cloned.1.call-done
  64.0 0.0 copy-start.1
  64.0 2.6 %fusion = f32[192,256]{1,0:T(8,128)S(1)} fusion(bf16[192,4096]{1,0:T(8,128)(2,1)S(1)} %pad_maximum_fusion, bf16[1024,4096]{1,0:T(8,128)(2,1)} %all-gather.4.cloned.1.call-done), kind=kOutput, calls=%fused_computation | convolution fusion | flops 402653184 | bytes 3866624 | tf_op jit(solution)/shard_map/dot_general | solution.py:43
  66.6 2.9 %fusion.2 = f32[192,256]{1,0:T(8,128)S(1)} fusion(bf16[192,4096]{1,0:T(8,128)(2,1)S(1)} %pad_maximum_fusion, bf16[1024,4096]{1,0:T(8,128)(2,1)} %all-gather.4.cloned.1.call-done), kind=kOutput, calls=%fused_computation.2 | convolution fusion | flops 402653184 | bytes 3866624 | tf_op jit(solution)/shard_map/dot_general | solution.py:43
  69.5 0.0 copy-done.1
  69.5 0.8 fusion.4
  70.3 0.8 fusion.6
  71.2 0.1 pad_maximum_fusion.2
  71.2 33.3 %all_to_all.35 = f32[32,24,256]{2,1,0:T(8,128)S(1)} all-to-all(f32[32,24,256]{2,1,0:T(8,128)S(1)} %bitcast.18), channel_id=1, replica_groups=mesh['feat_0'=4,'feat_1'=8,'dp_0'=4,'dp_1'=2] {'feat_0','feat_1'}, dimensions={0} | all-to-all | bytes 1572864 | tf_op jit(solution)/shard_map/all_to_all | solution.py:218
  104.5 0.1 reduce_sum.31
  104.6 0.1 broadcast_in_dim.14
  104.6 27.7 %all_to_all.36 = f32[32,24,256]{2,1,0:T(8,128)S(1)} all-to-all(f32[32,24,256]{2,1,0:T(8,128)S(1)} %broadcast_in_dim.14), channel_id=1, replica_groups=mesh['feat_0'=4,'feat_1'=8,'dp_0'=4,'dp_1'=2] {'feat_0','feat_1'}, dimensions={0} | all-to-all | bytes 1572864 | tf_op jit(solution)/shard_map/all_to_all | solution.py:218
  132.3 1.0 pad_maximum_fusion.1
  133.3 0.0 all-gather.6.cloned.1.call-update
  133.3 0.0 all-gather.8.cloned.1.call-done
  133.4 0.0 copy-start.2
  133.4 6.0 %fusion.8.sq_ref = f32[512,512]{1,0:T(8,128)S(1)} fusion(bf16[512,4096]{1,0:T(8,128)(2,1)} %param.5, bf16[512,4096]{1,0:T(8,128)(2,1)} %all-gather.8.cloned.1.call-done), kind=kOutput, calls=%fused_computation.13 | convolution fusion | flops 2147483648 | bytes 9437184 | tf_op jit(solution)/shard_map/dot_general | solution.py:43
  139.3 0.0 copy-done.2
  139.3 7.3 %fusion.9.sb_ref = f32[512,1024]{1,0:T(8,128)S(1)} fusion(bf16[512,4096]{1,0:T(8,128)(2,1)S(1)} %copy-done.2, bf16[1024,4096]{1,0:T(8,128)(2,1)} %all-gather.4.cloned.1.call-done), kind=kOutput, calls=%fused_computation.14 | convolution fusion | flops 4294967296 | bytes 14680064 | tf_op jit(solution)/shard_map/dot_general | solution.py:43
  146.7 25.5 %all-gather.6.cloned.1.call-done = f32[6208,256]{1,0:T(8,128)} async-done(((f32[776,256]{1,0:T(8,128)}), f32[6208,256]{1,0:T(8,128)}) %all-gather.6.cloned.1.call-update) | async-done | bytes 6357008 | tf_op jit(solution)/shard_map/all_gather | solution.py:241
  172.2 41.7 %solve.1 = bf16[512,512]{1,0:T(8,128)(2,1)S(1)} custom-call(f32[8,776,256]{2,1,0:T(8,128)} %bitcast.21, f32[512,1024]{1,0:T(8,128)S(1)} %fusion.9.sb_ref, f32[512,512]{1,0:T(8,128)S(1)} %fusion.8.sq_ref), custom_call_target="tpu_custom_call" | custom-call | flops 20000000000 | bytes 12000000 | tf_op jit(solution)/shard_map/solve/pallas_call | solution.py:196
  213.9 28.0 %all_to_all.37 = bf16[32,16,512]{2,1,0:T(8,128)(2,1)S(1)} all-to-all(bf16[32,16,512]{2,1,0:T(8,128)(2,1)S(1)} %bitcast.16), channel_id=1, replica_groups=mesh['feat_0'=4,'feat_1'=8,'dp_0'=4,'dp_1'=2] {'feat_0','feat_1'}, dimensions={0} | all-to-all | bytes 1048576 | tf_op jit(solution)/shard_map/all_to_all | solution.py:218
  241.9 0.7 convert_reduce_fusion
  (1 shorter events, 0.0 us)
Async XLA Ops:
  6.5 54.5 %copy-start = (bf16[128,4096]{1,0:T(8,128)(2,1)S(1)}, bf16[128,4096]{1,0:T(8,128)(2,1)}, u32[]{:S(2)}) copy-start(bf16[128,4096]{1,0:T(8,128)(2,1)} %param.4) | copy-start | bytes 3145732
  6.5 57.5 %all-gather.4.cloned.1.call-start = ((), (), s32[]{:S(2)}) async-start(), calls=%async_computation.4 | async-start | bytes 9437184 | tf_op jit(solution)/shard_map/all_gather | solution.py:223
  7.3 126.1 %all-gather.8.cloned.1.call-start = ((), (), s32[]{:S(2)}) async-start(), calls=%async_computation.6 | async-start | bytes 4718592 | tf_op jit(solution)/shard_map/all_gather | solution.py:242
  37.3 134.9 %all-gather.6.cloned.1.call-start = ((), (), s32[]{:S(2)}) async-start(), calls=%async_computation.5 | async-start | bytes 7151616 | tf_op jit(solution)/shard_map/all_gather | solution.py:241
  64.0 5.5 %copy-start.1 = (bf16[1024,4096]{1,0:T(8,128)(2,1)S(1)}, bf16[1024,4096]{1,0:T(8,128)(2,1)}, u32[]{:S(2)}) copy-start(bf16[1024,4096]{1,0:T(8,128)(2,1)} %all-gather.4.cloned.1.call-done) | copy-start | bytes 25165828
  133.4 6.0 %copy-start.2 = (bf16[512,4096]{1,0:T(8,128)(2,1)S(1)}, bf16[512,4096]{1,0:T(8,128)(2,1)}, u32[]{:S(2)}) copy-start(bf16[512,4096]{1,0:T(8,128)(2,1)} %param.5) | copy-start | bytes 12582916
Sparse Core Ops, SparseCore 0:
  9.2 54.7 all-gather.3
  65.9 34.7 all-gather.7
  133.4 38.6 all-gather.5
